TPU v7x, 512 devices: a whole 4x8x8 slice. The times are simulated.
512 devices in a mesh: pts: 64 (over y, x, core), tm: 8 (over z).
Axes of the slice: x: 4, y: 8, z: 8, core: 2. Of those that a mesh axis runs over, the one named last changes fastest.
Arguments:
- starting_location_factors: float32 [32768, 128], P('pts'), may hold values from -5 to 5
- starting_temporal_factors: float32 [8192, 128], P('tm'), may hold values from -5 to 5
- imposed_tension_record: float32 [32768, 8192], P('pts', 'tm'), may hold values from -10 to 10
- viscous_rate_factor: float32 [32768], P('pts'), may hold values from 0.2 to 1
- norton_power_law: float32 [32768], P('pts'), may hold values from 1.2 to 2.2
- space_inverse: float32 [128, 128], replicated, may hold values from -2 to 2
- time_inverse: float32 [128, 128], replicated, may hold values from -2 to 2
Outputs:
- space_out: float32 [32768, 128], P('pts')
- time_out: float32 [8192, 128], P('tm')
- misfit: float32 [2], replicated
All inputs are finite; a program needn't handle non-finite values.
Results may differ from a plain program's by a relative error of at most 0.0005.
Values sent between devices are 32-bit elements; how exact they have to be, the bound alone decides.
A program may use at most 64 MiB of HBM per device.

v0:
```python
import math
import jax
import jax.numpy as jnp
from jax import lax
from jax.sharding import PartitionSpec as P

ITERS = 2
highest = lax.Precision.HIGHEST


def viscous_pass(
    starting_location_factors,
    starting_temporal_factors,
    imposed_tension_record,
    viscous_rate_factor,
    norton_power_law,
):
    rank_scale = 1.0 / math.sqrt(starting_location_factors.shape[1])
    recon_field = (
        jnp.dot(starting_location_factors, starting_temporal_factors.T, precision=highest)
        * rank_scale
    )
    stress = imposed_tension_record - recon_field
    flow_rate = (
        viscous_rate_factor[:, None]
        * stress
        * jnp.power(stress * stress + 1e-06, 0.5 * (norton_power_law[:, None] - 1.0))
    )
    return (stress, flow_rate)


def shards(
    starting_location_factors,
    starting_temporal_factors,
    imposed_tension_record,
    viscous_rate_factor,
    norton_power_law,
    space_inverse,
    time_inverse,
):
    pts_count = lax.axis_size("pts")
    instant_count = lax.axis_size("tm")
    point_total = starting_location_factors.shape[0] * pts_count
    instant_total = starting_temporal_factors.shape[0] * instant_count
    share_rows = starting_temporal_factors.shape[0] // pts_count
    residual_record = []
    for sweep in range(ITERS):
        stress, flow_rate = viscous_pass(
            starting_location_factors,
            starting_temporal_factors,
            imposed_tension_record,
            viscous_rate_factor,
            norton_power_law,
        )
        residual_energy = jnp.sum(stress * stress)
        time_part = lax.dot_general(
            flow_rate, starting_location_factors, (((0,), (0,)), ((), ())), precision=highest
        )
        time_sum = lax.psum(time_part, "pts")
        temporal_factors_before_rescale = jnp.dot(time_sum, time_inverse, precision=highest)
        own_start = lax.axis_index("pts") * share_rows
        own_block = lax.dynamic_slice_in_dim(
            temporal_factors_before_rescale, own_start, share_rows, 0
        )
        temporal_magnitude_quad = jnp.sum(own_block * own_block, axis=0)
        space_part = jnp.dot(flow_rate, starting_temporal_factors, precision=highest)
        space_sum = lax.psum(space_part, "tm")
        space_raw = jnp.dot(space_sum, space_inverse, precision=highest)
        space_sq = jnp.sum(space_raw * space_raw, axis=0)
        space_sq = lax.psum(space_sq, "pts")
        temporal_magnitude_quad = lax.psum(temporal_magnitude_quad, ("pts", "tm"))
        residual_energy = lax.psum(residual_energy, ("pts", "tm"))
        starting_location_factors = space_raw / jnp.sqrt(space_sq / point_total + 1e-06)
        updated_time_modes = temporal_factors_before_rescale / jnp.sqrt(
            temporal_magnitude_quad / instant_total + 1e-06
        )
        starting_temporal_factors = updated_time_modes
        residual_record.append(residual_energy / (point_total * instant_total))
    return (starting_location_factors, starting_temporal_factors, jnp.stack(residual_record))


def solution(mesh):
    return jax.shard_map(
        shards,
        mesh=mesh,
        in_specs=(P("pts", None), P("tm", None), P("pts", "tm"), P("pts"), P("pts"), P(), P()),
        out_specs=(P("pts", None), P("tm", None), P()),
        check_vma=False,
    )
```

profile of v0, /device:TPU:1, one launch (start us, length us, event | category | flops | bytes accessed | tf_op | source)
XLA Modules:
  0.0 881.4 jit_solution(14366667147604201860)
XLA Ops:
  7.2 0.0 copy-start
  7.2 0.0 all-reduce.8.cloned.1.call-start
  7.2 0.7 add_multiply_fusion
  8.0 0.3 copy-done
  8.2 0.0 copy-start.4
  8.2 0.0 copy-start.7
  8.2 4.5 multiply_reduce_fusion.1
  12.7 0.0 copy-start.3
  12.7 1.3 copy-done.3
  14.1 0.0 copy-done.4
  14.1 0.0 copy-done.7
  14.1 7.1 fusion
  21.2 0.0 copy-start.5
  21.2 0.0 all-reduce.8.cloned.1.call-update
  21.2 0.0 copy-start.6
  21.3 0.0 copy-start.1
  21.3 0.2 all-reduce.6.cloned.1.call-start
  21.5 7.3 fusion.1
  28.8 0.0 all-reduce.6.cloned.1.call-update
  28.8 0.0 all-reduce.12.cloned.1.call-start
  28.9 189.0 %all-reduce.8.cloned.1.call-done = f32[1024,128]{1,0:T(8,128)} async-done(((f32[1024,128]{1,0:T(8,128)}), f32[1024,128]{1,0:T(8,128)}) %all-reduce.8.cloned.1.call-update) | async-done | bytes 524304 | tf_op jit(solution)/shard_map/psum | solution.py:59
  217.9 0.0 copy-done.5
  217.9 1.6 fusion.20
  219.5 99.1 %psum.73 = f32[128]{0:T(128)S(1)} all-reduce(f32[128]{0:T(128)S(1)} %multiply_reduce_fusion.5), channel_id=1, replica_groups=mesh['pts'=64,'tm'=8] {'pts','tm'}, use_global_device_ids=true, to_apply=%region_5.0 | all-reduce | flops 128 | bytes 1024 | tf_op jit(solution)/shard_map/psum | solution.py:71
  318.6 0.0 all-reduce.6.cloned.1.call-done
  318.6 0.0 copy-done.6
  318.6 1.3 multiply_reduce_fusion.3
  319.9 125.1 %psum.71 = f32[128]{0:T(128)} all-reduce(f32[128]{0:T(128)S(1)} %get-tuple-element.6), channel_id=1, replica_groups=mesh['pts'=64,'tm'=8] {'pts'}, use_global_device_ids=true, to_apply=%region_2.0 | all-reduce | flops 128 | bytes 1024 | tf_op jit(solution)/shard_map/psum | solution.py:70
  445.0 0.7 add_sqrt_fusion.3
  445.7 0.0 copy-done.1
  445.7 2.8 multiply_reduce_fusion
  448.5 0.0 copy-start.2
  448.5 1.3 copy-done.2
  449.9 7.1 fusion.2
  457.0 0.0 all-reduce.12.cloned.1.call-update
  457.0 0.3 all-reduce.10.cloned.1.call-start
  457.3 7.3 fusion.3
  464.6 0.0 all-reduce.10.cloned.1.call-update
  464.6 180.4 %all-reduce.12.cloned.1.call-done = f32[1024,128]{1,0:T(8,128)} async-done(((f32[1024,128]{1,0:T(8,128)}), f32[1024,128]{1,0:T(8,128)}) %all-reduce.12.cloned.1.call-update) | async-done | bytes 524304 | tf_op jit(solution)/shard_map/psum | solution.py:59
  645.0 1.6 fusion.21
  646.6 99.2 %all-reduce = (f32[128]{0:T(128)S(1)}, f32[]{:T(128)}, f32[]{:T(128)}) all-reduce(f32[128]{0:T(128)S(1)} %multiply_reduce_fusion.4, f32[]{:T(128)} %get-tuple-element.10, f32[]{:T(128)} %get-tuple-element.12), channel_id=1, replica_groups=mesh['pts'=64,'tm'=8] {'pts','tm'}, use_global_device_ids=true, to_apply=%region_11.0 | all-reduce | flops 130 | bytes 1040 | tf_op jit(solution)/shard_map/psum | solution.py:71
  747.1 0.8 broadcast_divide_fusion
  748.0 0.0 all-reduce.10.cloned.1.call-done
  748.0 1.3 multiply_reduce_fusion.2
  749.3 124.2 %psum.75 = f32[128]{0:T(128)S(1)} all-reduce(f32[128]{0:T(128)S(1)} %get-tuple-element.8), channel_id=1, replica_groups=mesh['pts'=64,'tm'=8] {'pts'}, use_global_device_ids=true, to_apply=%region_8.0 | all-reduce | flops 128 | bytes 1024 | tf_op jit(solution)/shard_map/psum | solution.py:70
  873.5 0.6 pad_maximum_fusion
  874.1 0.7 broadcast_divide_fusion.4
  (5 shorter events, 0.1 us)
Async XLA Ops:
  7.2 1.1 copy-start
  7.2 210.7 %all-reduce.8.cloned.1.call-start = ((), (), s32[]{:S(2)}) async-start(), calls=%async_computation.1 | async-start | bytes 1048576 | tf_op jit(solution)/shard_map/psum | solution.py:59
  8.2 5.9 copy-start.4
  8.2 5.9 copy-start.7
  12.7 1.4 copy-start.3
  21.2 196.7 %copy-start.5 = (f32[128,128]{1,0:T(8,128)S(1)}, f32[128,128]{1,0:T(8,128)}, u32[]{:S(2)}) copy-start(f32[128,128]{1,0:T(8,128)} %param.13) | copy-start | bytes 196612
  21.2 297.4 %copy-start.6 = (f32[128,128]{1,0:T(8,128)S(1)}, f32[128,128]{1,0:T(8,128)}, u32[]{:S(2)}) copy-start(f32[128,128]{1,0:T(8,128)} %param.12) | copy-start | bytes 196612
  21.3 424.4 %copy-start.1 = (f32[512,1024]{1,0:T(8,128)S(1)}, f32[512,1024]{1,0:T(8,128)}, u32[]{:S(2)}) copy-start(f32[512,1024]{1,0:T(8,128)} %param.9) | copy-start | bytes 6291460
  21.3 297.3 %all-reduce.6.cloned.1.call-start = ((), (), s32[]{:S(2)}) async-start(), calls=%async_computation | async-start | bytes 524288 | tf_op jit(solution)/shard_map/psum | solution.py:67
  28.8 616.1 %all-reduce.12.cloned.1.call-start = ((), (), s32[]{:S(2)}) async-start(), calls=%async_computation.3 | async-start | bytes 1048576 | tf_op jit(solution)/shard_map/psum | solution.py:59
  448.5 1.4 copy-start.2
  457.0 290.9 %all-reduce.10.cloned.1.call-start = ((), (), s32[]{:S(2)}) async-start(), calls=%async_computation.2 | async-start | bytes 524288 | tf_op jit(solution)/shard_map/psum | solution.py:67
Sparse Core Ops, SparseCore 0:
  21.4 196.4 all-reduce.7
  220.8 73.5 all-reduce.5
  457.1 187.8 all-reduce.11
  647.8 73.5 all-reduce.9
where the time goes:
time: 882 us; the launch traced here: 881 us
  blocking collectives  448 us (51%)
  waiting for transfers between devices  369 us (42%)
  matrix products  42 us (5%)
  between operations  15.1 us (2%)
    psum x2, waiting for transfers between devices, shards(): time_sum = lax.psum(time_part, 'pts')  369 us
    psum x2, blocking collectives, shards(): space_sq = lax.psum(space_sq, 'pts')  249 us
    psum x2, blocking collectives, shards(): temporal_magnitude_quad = lax.psum(temporal_magnitude_quad, ('pts', 'tm'))  198 us
  transfers between devices with their start and end apart: 4, of which 2 were waited for; matrix products, arithmetic and copies ran while one was open for 2% of the time, Pallas kernels for 0%

commit v1 on v0

--- a/solution.py
+++ b/solution.py
@@ -6,6 +6,7 @@
 
 ITERS = 2
 highest = lax.Precision.HIGHEST
+pieces_all_drive = lambda array_in: lax.psum(lax.psum(array_in, axis_name="tm"), axis_name="pts")
 
 
 def viscous_pass(
@@ -68,7 +69,7 @@
         space_raw = jnp.dot(space_sum, space_inverse, precision=highest)
         space_sq = jnp.sum(space_raw * space_raw, axis=0)
         space_sq = lax.psum(space_sq, "pts")
-        temporal_magnitude_quad = lax.psum(temporal_magnitude_quad, ("pts", "tm"))
+        temporal_magnitude_quad = pieces_all_drive(temporal_magnitude_quad)
         residual_energy = lax.psum(residual_energy, ("pts", "tm"))
         starting_location_factors = space_raw / jnp.sqrt(space_sq / point_total + 1e-06)
         updated_time_modes = temporal_factors_before_rescale / jnp.sqrt(

time: 882 us -> 838 us (0.950)
  blocking collectives: 448 us -> 384 us
  waiting for transfers between devices: 369 us -> 390 us
    psum x2 -> x1, blocking collectives: 249 us -> 129 us  [shards(): space_sq = lax.psum(space_sq, 'pts')]
    psum x2, waiting for transfers between devices: 0.01 us -> 120 us  [shards(): space_sum = lax.psum(space_part, 'tm')]
    psum x2, waiting for transfers between devices: 369 us -> 270 us  [shards(): time_sum = lax.psum(time_part, 'pts')]
    psum x2 -> x4, blocking collectives: 198 us -> 256 us  [the longest x1 129 us: lax.psum(lax.psum(array_in, axis_name='tm'), axis_name='pts')]
  transfers between devices with their start and end apart: 4 -> 4, of which waited for: 2 -> 4; matrix products, arithmetic and copies ran while one was open for 2% -> 2% of each run, Pallas kernels for 0% -> 0%
where the time goes in v1:
time: 838 us
  waiting for transfers between devices  390 us (47%)
  blocking collectives  384 us (46%)
  matrix products  42 us (5%)
  between operations  15.1 us (2%)
    psum x2, waiting for transfers between devices, shards(): time_sum = lax.psum(time_part, 'pts')  270 us
    psum x1, blocking collectives, lax.psum(lax.psum(array_in, axis_name='tm'), axis_name='pts')  129 us
    psum x1, blocking collectives, shards(): space_sq = lax.psum(space_sq, 'pts')  129 us
    psum x2, waiting for transfers between devices, shards(): space_sum = lax.psum(space_part, 'tm')  120 us
    psum x1, blocking collectives, shards(): residual_energy = lax.psum(residual_energy, ('pts', 'tm'))  97.4 us
    psum x2, blocking collectives, lax.psum(array_in, axis_name='tm')  29.2 us
  transfers between devices with their start and end apart: 4, of which 4 were waited for; matrix products, arithmetic and copies ran while one was open for 2% of the time, Pallas kernels for 0%

profile of v1, /device:TPU:1, one launch (start us, length us, event | category | flops | bytes accessed | tf_op | source)
XLA Modules:
  0.0 837.6 jit_solution(599517991562146468)
XLA Ops:
  7.2 0.0 copy-start
  7.2 0.0 all-reduce.10.cloned.1.call-start
  7.2 0.7 add_multiply_fusion
  8.0 0.3 copy-done
  8.2 0.0 copy-start.4
  8.2 0.0 copy-start.7
  8.2 4.5 multiply_reduce_fusion.1
  12.7 0.0 copy-start.3
  12.7 1.3 copy-done.3
  14.1 0.0 copy-done.4
  14.1 0.0 copy-done.7
  14.1 7.1 fusion
  21.2 0.0 copy-start.5
  21.2 0.0 all-reduce.10.cloned.1.call-update
  21.2 0.0 copy-start.6
  21.3 0.0 copy-start.1
  21.3 0.2 all-reduce.8.cloned.1.call-start
  21.5 7.3 fusion.1
  28.8 0.0 all-reduce.8.cloned.1.call-update
  28.8 0.0 all-reduce.14.cloned.1.call-start
  28.9 189.0 %all-reduce.10.cloned.1.call-done = f32[1024,128]{1,0:T(8,128)} async-done(((f32[1024,128]{1,0:T(8,128)}), f32[1024,128]{1,0:T(8,128)}) %all-reduce.10.cloned.1.call-update) | async-done | bytes 524304 | tf_op jit(solution)/shard_map/psum | solution.py:60
  217.9 0.0 copy-done.5
  217.9 1.6 fusion.20
  219.5 14.8 %psum.87 = f32[128]{0:T(128)} all-reduce(f32[128]{0:T(128)S(1)} %multiply_reduce_fusion.5), channel_id=1, replica_groups=mesh['pts'=64,'tm'=8] {'tm'}, use_global_device_ids=true, to_apply=%region_5.0 | all-reduce | flops 128 | bytes 1024 | tf_op jit(solution)/shard_map/psum | solution.py:9
  234.4 59.7 %all-reduce.8.cloned.1.call-done = f32[512,128]{1,0:T(8,128)} async-done(((f32[512,128]{1,0:T(8,128)}), f32[512,128]{1,0:T(8,128)}) %all-reduce.8.cloned.1.call-update) | async-done | bytes 262160 | tf_op jit(solution)/shard_map/psum | solution.py:68
  294.0 0.0 copy-done.6
  294.0 1.3 multiply_reduce_fusion.3
  295.4 129.1 %all-reduce.2 = (f32[128]{0:T(128)S(1)}, f32[128]{0:T(128)S(1)}) all-reduce(f32[128]{0:T(128)} %psum.87, f32[128]{0:T(128)S(1)} %get-tuple-element.9), channel_id=1, replica_groups=mesh['pts'=64,'tm'=8] {'pts'}, use_global_device_ids=true, to_apply=%region_6.0 | all-reduce | flops 256 | bytes 2048 | tf_op jit(solution)/shard_map/psum | solution.py:9
  424.4 0.0 copy-done.1
  424.4 0.0 copy-start.8
  424.5 2.8 multiply_reduce_fusion
  427.3 1.3 copy-done.2
  428.6 0.0 copy-done.8
  428.6 7.1 fusion.2
  435.8 0.0 all-reduce.14.cloned.1.call-update
  435.8 0.0 all-reduce.12.cloned.1.call-start
  435.8 97.4 %all-reduce = (f32[]{:T(128)}, f32[]{:T(128)}) all-reduce(f32[]{:T(128)} %get-tuple-element.13, f32[]{:T(128)} %get-tuple-element.15), channel_id=1, replica_groups=mesh['pts'=64,'tm'=8] {'pts','tm'}, use_global_device_ids=true, to_apply=%region_17.0 | all-reduce | flops 2 | bytes 16 | tf_op jit(solution)/shard_map/psum | solution.py:73
  534.5 7.3 fusion.3
  541.8 0.0 all-reduce.12.cloned.1.call-update
  541.8 0.6 pad_maximum_fusion
  542.4 80.9 %all-reduce.14.cloned.1.call-done = f32[1024,128]{1,0:T(8,128)} async-done(((f32[1024,128]{1,0:T(8,128)}), f32[1024,128]{1,0:T(8,128)}) %all-reduce.14.cloned.1.call-update) | async-done | bytes 524304 | tf_op jit(solution)/shard_map/psum | solution.py:60
  623.3 1.6 fusion.21
  624.9 14.4 %psum.92 = f32[128]{0:T(128)S(1)} all-reduce(f32[128]{0:T(128)S(1)} %multiply_reduce_fusion.4), channel_id=1, replica_groups=mesh['pts'=64,'tm'=8] {'tm'}, use_global_device_ids=true, to_apply=%region_12.0 | all-reduce | flops 128 | bytes 1024 | tf_op jit(solution)/shard_map/psum | solution.py:9
  639.3 60.1 %all-reduce.12.cloned.1.call-done = f32[512,128]{1,0:T(8,128)} async-done(((f32[512,128]{1,0:T(8,128)}), f32[512,128]{1,0:T(8,128)}) %all-reduce.12.cloned.1.call-update) | async-done | bytes 262160 | tf_op jit(solution)/shard_map/psum | solution.py:68
  699.4 1.3 multiply_reduce_fusion.2
  700.7 128.7 %all-reduce.1 = (f32[128]{0:T(128)S(1)}, f32[128]{0:T(128)S(1)}) all-reduce(f32[128]{0:T(128)S(1)} %get-tuple-element.11, f32[128]{0:T(128)S(1)} %psum.92), channel_id=1, replica_groups=mesh['pts'=64,'tm'=8] {'pts'}, use_global_device_ids=true, to_apply=%region_9.0 | all-reduce | flops 256 | bytes 2048 | tf_op jit(solution)/shard_map/psum | solution.py:71
  829.4 0.8 broadcast_divide_fusion
  830.3 0.7 broadcast_divide_fusion.4
  (6 shorter events, 0.1 us)
Async XLA Ops:
  7.2 1.1 copy-start
  7.2 210.7 %all-reduce.10.cloned.1.call-start = ((), (), s32[]{:S(2)}) async-start(), calls=%async_computation.1 | async-start | bytes 1048576 | tf_op jit(solution)/shard_map/psum | solution.py:60
  8.2 5.9 copy-start.4
  8.2 5.9 copy-start.7
  12.7 1.4 copy-start.3
  21.2 196.7 %copy-start.5 = (f32[128,128]{1,0:T(8,128)S(1)}, f32[128,128]{1,0:T(8,128)}, u32[]{:S(2)}) copy-start(f32[128,128]{1,0:T(8,128)} %param.13) | copy-start | bytes 196612
  21.2 272.8 %copy-start.6 = (f32[128,128]{1,0:T(8,128)S(1)}, f32[128,128]{1,0:T(8,128)}, u32[]{:S(2)}) copy-start(f32[128,128]{1,0:T(8,128)} %param.12) | copy-start | bytes 196612
  21.3 403.2 %copy-start.1 = (f32[512,1024]{1,0:T(8,128)S(1)}, f32[512,1024]{1,0:T(8,128)}, u32[]{:S(2)}) copy-start(f32[512,1024]{1,0:T(8,128)} %param.9) | copy-start | bytes 6291460
  21.3 272.8 %all-reduce.8.cloned.1.call-start = ((), (), s32[]{:S(2)}) async-start(), calls=%async_computation | async-start | bytes 524288 | tf_op jit(solution)/shard_map/psum | solution.py:68
  28.8 594.5 %all-reduce.14.cloned.1.call-start = ((), (), s32[]{:S(2)}) async-start(), calls=%async_computation.3 | async-start | bytes 1048576 | tf_op jit(solution)/shard_map/psum | solution.py:60
  424.4 4.2 copy-start.8
  427.3 1.4 copy-start.2
  435.8 263.6 %all-reduce.12.cloned.1.call-start = ((), (), s32[]{:S(2)}) async-start(), calls=%async_computation.2 | async-start | bytes 524288 | tf_op jit(solution)/shard_map/psum | solution.py:68
Sparse Core Ops, SparseCore 0:
  21.4 196.4 all-reduce.9
  220.8 73.2 all-reduce.7
  435.9 187.3 all-reduce.13
  626.2 73.1 all-reduce.11
